TPU v7x, 32 devices: a whole 2x2x4 slice. The times are simulated.
32 devices in a mesh: seq: 16 (over z, y, x), chan: 2 (over core).
Axes of the slice: x: 2, y: 2, z: 4, core: 2. Of those that a mesh axis runs over, the one named last changes fastest.
Arguments:
- values: bfloat16 [256, 8192], P('chan', 'seq'), may hold values from -6 to 6
- gate_one: bfloat16 [256, 8192], P('chan', 'seq'), may hold values from -6 to 6
- gate_two: bfloat16 [256, 8192], P('chan', 'seq'), may hold values from -6 to 6
- filter_one: float32 [256, 8192], P('chan', 'seq'), may hold values from -1 to 1
- filter_two: float32 [256, 8192], P('chan', 'seq'), may hold values from -1 to 1
- skip_one: float32 [256], P('chan'), may hold values from -1 to 1
- skip_two: float32 [256], P('chan'), may hold values from -1 to 1
- mix_weight: bfloat16 [256, 256], P(None, 'chan'), may hold values from -0.375 to 0.375
Outputs:
- mixed: bfloat16 [256, 8192], P('chan', 'seq')
All inputs are finite; a program needn't handle non-finite values.
Results may differ from a plain program's by a relative error of at most 0.0051.
Values may be sent and summed in bfloat16 or wider, within the bound.
A program may use at most 64 MiB of HBM per device.

v0:
```python
import math
import jax
import jax.numpy as jnp
from jax import lax
from jax.sharding import PartitionSpec as P

FOLD = 512
exact_mode = lax.Precision.HIGHEST


def angle_of(integers, modulus):
    return integers.astype(jnp.float32) * (2.0 * math.pi / modulus)


def fourier_rows(half_rows, column_count, period):
    row_index = lax.iota(jnp.int32, half_rows)[:, None]
    column_index = lax.iota(jnp.int32, column_count)[None, :]
    angles = angle_of(row_index * column_index % period, period)
    cosine = jnp.cos(angles)
    sine_tab = jnp.sin(angles)
    alternate = (1 - 2 * (row_index % 2)).astype(jnp.float32)
    sine_tab = jnp.where(column_index == 0, -alternate, sine_tab)
    return (cosine, sine_tab)


def fold_tables():
    points = lax.iota(jnp.int32, FOLD)
    angles = angle_of(points[:, None] * points[None, :] % FOLD, FOLD)
    return (jnp.cos(angles), jnp.sin(angles))


def spectra(columns_in):
    narrow = columns_in.shape[1]
    half_rows = columns_in.shape[2]
    period = 2 * half_rows
    modulus = period * FOLD
    seq_index = lax.axis_index("seq")
    cosine, sine_tab = fourier_rows(half_rows, half_rows, period)
    real_part = jnp.einsum("kra,ac->krc", columns_in, cosine, precision=exact_mode)
    imag_part = -jnp.einsum("kra,ac->krc", columns_in, sine_tab, precision=exact_mode)
    points_glob = seq_index * narrow + lax.iota(jnp.int32, narrow)
    column_index = lax.iota(jnp.int32, cosine.shape[1])
    angles = angle_of(points_glob[:, None] * column_index[None, :] % modulus, modulus)
    turn_cos = jnp.cos(angles)
    turn_sin = jnp.sin(angles)
    real_twist = real_part * turn_cos + imag_part * turn_sin
    imag_twist = imag_part * turn_cos - real_part * turn_sin
    real_recv, imag_recv = (
        lax.all_to_all(real_twist, "seq", split_axis=2, concat_axis=1, tiled=True),
        lax.all_to_all(imag_twist, "seq", split_axis=2, concat_axis=1, tiled=True),
    )
    row_count = real_recv.shape[2]
    is_leader = seq_index == 0
    spare_row = imag_recv
    phases = angle_of(lax.iota(jnp.int32, FOLD), 2 * FOLD)[None, :, None]
    row_mask = ((lax.iota(jnp.int32, row_count) == 0) & is_leader)[None, None, :]
    imag_recv = jnp.where(row_mask, 0.0, imag_recv)
    real_recv = jnp.concatenate([real_recv, spare_row * jnp.cos(phases)], axis=2)
    imag_recv = jnp.concatenate([imag_recv, -spare_row * jnp.sin(phases)], axis=2)
    rows_glob = jnp.concatenate(
        [
            seq_index * row_count + lax.iota(jnp.int32, row_count),
            jnp.full((1,), half_rows, jnp.int32),
        ]
    )
    cosine_q, sine_q = fold_tables()
    first_prod = jnp.einsum("kbr,bd->krd", real_recv + imag_recv, cosine_q, precision=exact_mode)
    second_prod = jnp.einsum("kbr,bd->krd", real_recv, -sine_q - cosine_q, precision=exact_mode)
    third_prod = jnp.einsum("kbr,bd->krd", imag_recv, cosine_q - sine_q, precision=exact_mode)
    return (first_prod - third_prod, first_prod + second_prod, rows_glob)


def inverse(spec_real, spectrum_imaginary, rows_glob, half_rows):
    period = 2 * half_rows
    modulus = period * FOLD
    seq_index = lax.axis_index("seq")
    cosine_q, sine_q = fold_tables()
    first_prod = jnp.einsum(
        "krd,db->kbr", spec_real + spectrum_imaginary, cosine_q, precision=exact_mode
    )
    second_prod = jnp.einsum("krd,db->kbr", spec_real, sine_q - cosine_q, precision=exact_mode)
    third_prod = jnp.einsum(
        "krd,db->kbr", spectrum_imaginary, cosine_q + sine_q, precision=exact_mode
    )
    real_part = first_prod - third_prod
    imag_part = first_prod + second_prod
    angles = angle_of(lax.iota(jnp.int32, FOLD)[:, None] * rows_glob[None, :] % modulus, modulus)
    turn_cos = jnp.cos(angles)
    turn_sin = jnp.sin(angles)
    real_twist = real_part * turn_cos - imag_part * turn_sin
    imag_twist = real_part * turn_sin + imag_part * turn_cos
    row_count = real_twist.shape[2] - 1
    row_mask = ((lax.iota(jnp.int32, row_count) == 0) & (seq_index == 0))[None, None, :]
    imag_send = jnp.where(row_mask, real_twist[:, :, row_count:], imag_twist[:, :, :row_count])
    real_recv, imag_recv = (
        lax.all_to_all(
            real_twist[:, :, :row_count], "seq", split_axis=1, concat_axis=2, tiled=True
        ),
        lax.all_to_all(imag_send, "seq", split_axis=1, concat_axis=2, tiled=True),
    )
    cosine, sine_tab = fourier_rows(half_rows, half_rows, period)
    coefficient_matrix = jnp.where(lax.iota(jnp.int32, half_rows) == 0, 1.0, 2.0).astype(
        jnp.float32
    )[None, :]
    cosine = cosine * coefficient_matrix
    sine_tab = sine_tab * coefficient_matrix
    result = jnp.einsum("kbc,ac->kba", real_recv, cosine, precision=exact_mode)
    result = result - jnp.einsum("kbc,ac->kba", imag_recv, sine_tab, precision=exact_mode)
    return result / modulus


def convolve(value_real, value_imag, filter_real, filter_imag, rows_glob, half_rows):
    prod_real = value_real * filter_real - value_imag * filter_imag
    prod_imag = value_real * filter_imag + value_imag * filter_real
    return inverse(prod_real, prod_imag, rows_glob, half_rows)


def per_device(values, gate_one, gate_two, filter_one, filter_two, skip_one, skip_two, mix_weight):
    channels, tokens = values.shape
    blocks = tokens // FOLD

    def columns(source):
        return jnp.swapaxes(source.reshape(channels, blocks, FOLD), 1, 2)

    def from_columns(result_cols):
        return jnp.swapaxes(result_cols, 1, 2).reshape(channels, tokens)

    def to_tokens(result_cols):
        return from_columns(
            lax.all_to_all(result_cols, "seq", split_axis=2, concat_axis=1, tiled=True)
        )

    values_cols = lax.all_to_all(columns(values), "seq", split_axis=1, concat_axis=2, tiled=True)
    filter_cols = (
        lax.all_to_all(columns(filter_one), "seq", split_axis=1, concat_axis=2, tiled=True),
        lax.all_to_all(columns(filter_two), "seq", split_axis=1, concat_axis=2, tiled=True),
    )
    values_wide = values_cols.astype(jnp.float32)
    half_rows = values_wide.shape[2]
    stacked = jnp.concatenate([values_wide, filter_cols[0], filter_cols[1]], axis=0)
    spec_real, spectrum_imaginary, rows_glob = spectra(stacked)
    conv_one = convolve(
        spec_real[:channels],
        spectrum_imaginary[:channels],
        spec_real[channels : 2 * channels],
        spectrum_imaginary[channels : 2 * channels],
        rows_glob,
        half_rows,
    )
    filter_two_real = spec_real[2 * channels :]
    filter_two_imag = spectrum_imaginary[2 * channels :]
    conv_tokens = to_tokens(conv_one)
    gated = gate_one.astype(jnp.float32) * (
        conv_tokens + skip_one[:, None] * values.astype(jnp.float32)
    )
    gated_cols = lax.all_to_all(columns(gated), "seq", split_axis=1, concat_axis=2, tiled=True)
    second_real, second_imag, restored_lines = spectra(gated_cols)
    conv_two = convolve(
        second_real, second_imag, filter_two_real, filter_two_imag, restored_lines, half_rows
    )
    second_tokens = to_tokens(conv_two)
    mixed_in = (gate_two.astype(jnp.float32) * (second_tokens + skip_two[:, None] * gated)).astype(
        jnp.bfloat16
    )
    summed = jnp.einsum(
        "de,dt->et",
        mix_weight,
        lax.all_gather(mixed_in, "chan", axis=0, tiled=True),
        preferred_element_type=jnp.float32,
    )
    return jax.nn.silu(summed).astype(jnp.bfloat16)


def solution(mesh):
    return jax.shard_map(
        per_device,
        mesh=mesh,
        in_specs=(
            P("chan", "seq"),
            P("chan", "seq"),
            P("chan", "seq"),
            P("chan", "seq"),
            P("chan", "seq"),
            P("chan"),
            P("chan"),
            P(None, "chan"),
        ),
        out_specs=P("chan", "seq"),
        check_vma=False,
    )
```

profile of v0, /device:TPU:0, one launch (start us, length us, event | category | flops | bytes accessed | tf_op | source)
XLA Modules:
  0.0 290.9 jit_solution(13032931578427769664)
XLA Ops:
  3.7 8.3 %all-to-all-start = ((bf16[16,2,2048]{2,1,0:T(2,128)(2,1)}), bf16[16,2,2048]{2,1,0:T(2,128)(2,1)S(1)}, u32[]{:S(2)}, u32[]{:S(2)}) async-start(bf16[16,2,2048]{2,1,0:T(2,128)(2,1)} %reshape.345), calls=%async_computation | async-start | bytes 262144 | tf_op jit(solution)/shard_map/all_to_all | solution.py:133
  13.9 6.0 %all-to-all-done = bf16[16,2,2048]{2,1,0:T(2,128)(2,1)S(1)} async-done(((bf16[16,2,2048]{2,1,0:T(2,128)(2,1)}), bf16[16,2,2048]{2,1,0:T(2,128)(2,1)S(1)}, u32[]{:S(2)}, u32[]{:S(2)}) %all-to-all-start) | async-done | bytes 131104 | tf_op jit(solution)/shard_map/all_to_all | solution.py:133
  24.3 7.6 %all-to-all-done.2 = f32[128,512,1]{0,2,1:T(1,128)S(1)} async-done(((f32[128,512,1]{0,2,1:T(1,128)}), f32[128,512,1]{0,2,1:T(1,128)S(1)}, u32[]{:S(2)}, u32[]{:S(2)}) %all-to-all-start.2) | async-done | bytes 262176 | tf_op jit(solution)/shard_map/all_to_all | solution.py:136
  31.9 3.7 %all-to-all-start.1 = ((f32[128,512,1]{0,2,1:T(1,128)}), f32[128,512,1]{0,2,1:T(1,128)S(1)}, u32[]{:S(2)}, u32[]{:S(2)}) async-start(f32[128,512,1]{0,2,1:T(1,128)} %bitcast.5), calls=%async_computation.1 | async-start | bytes 524288 | tf_op jit(solution)/shard_map/all_to_all | solution.py:135
  36.2 8.4 %all-to-all-done.1 = f32[128,512,1]{0,2,1:T(1,128)S(1)} async-done(((f32[128,512,1]{0,2,1:T(1,128)}), f32[128,512,1]{0,2,1:T(1,128)S(1)}, u32[]{:S(2)}, u32[]{:S(2)}) %all-to-all-start.1) | async-done | bytes 262176 | tf_op jit(solution)/shard_map/all_to_all | solution.py:135
  47.9 3.6 %all-to-all-start.4 = ((f32[384,32,16]{0,1,2:T(8,128)}), f32[384,32,16]{0,1,2:T(8,128)S(1)}, u32[]{:S(2)}, u32[]{:S(2)}) async-start(f32[384,32,16]{0,1,2:T(8,128)} %copy.119), calls=%async_computation.4 | async-start | bytes 1572864 | tf_op jit(solution)/shard_map/all_to_all | solution.py:50
  52.6 17.7 %all-to-all-done.4 = f32[384,32,16]{0,1,2:T(8,128)S(1)} async-done(((f32[384,32,16]{0,1,2:T(8,128)}), f32[384,32,16]{0,1,2:T(8,128)S(1)}, u32[]{:S(2)}, u32[]{:S(2)}) %all-to-all-start.4) | async-done | bytes 786464 | tf_op jit(solution)/shard_map/all_to_all | solution.py:50
  70.4 5.1 %all-to-all-start.3 = ((f32[384,32,16]{0,1,2:T(8,128)}), f32[384,32,16]{0,1,2:T(8,128)S(1)}, u32[]{:S(2)}, u32[]{:S(2)}) async-start(f32[384,32,16]{0,1,2:T(8,128)} %copy.118), calls=%async_computation.3 | async-start | bytes 1572864 | tf_op jit(solution)/shard_map/all_to_all | solution.py:49
  76.1 17.9 %all-to-all-done.3 = f32[384,32,16]{0,1,2:T(8,128)S(1)} async-done(((f32[384,32,16]{0,1,2:T(8,128)}), f32[384,32,16]{0,1,2:T(8,128)S(1)}, u32[]{:S(2)}, u32[]{:S(2)}) %all-to-all-start.3) | async-done | bytes 786464 | tf_op jit(solution)/shard_map/all_to_all | solution.py:49
  94.5 6.5 %fusion = f32[384,2,512]{2,0,1:T(8,128)S(1)} fusion(f32[384,512,1]{1,0,2:T(8,128)S(1)} %get-tuple-element.16, f32[384,512,1]{1,0,2:T(8,128)S(1)} %get-tuple-element.17, f32[384,512,1]{1,0,2:T(8,128)S(1)} %get-tuple-element.15, f32[384,512,1]{1,0,2:T(8,128)S(1)} %copy.121), kind=kOutput, calls=%fused_computation.2 | convolution fusion | flops 2420768768 | bytes 4718592 | tf_op jit(solution)/shard_map/kbr,bd->krd/dot_general | solution.py:67
  101.0 7.1 %convolution_subtract_fusion = f32[384,2,512]{2,0,1:T(8,128)S(1)} fusion(f32[384,2,512]{2,0,1:T(8,128)S(1)} %fusion, f32[384,512,1]{1,0,2:T(8,128)S(1)} %get-tuple-element.16, f32[384,512,1]{1,0,2:T(8,128)S(1)} %get-tuple-element.17), kind=kOutput, calls=%fused_computation.8 | convolution fusion | flops 2420637696 | bytes 4718592 | tf_op jit(solution)/shard_map/kbr,bd->krd/dot_general | solution.py:69
  108.1 6.9 %convolution_add_fusion = f32[384,2,512]{2,0,1:T(8,128)S(1)} fusion(f32[384,2,512]{2,0,1:T(8,128)S(1)} %fusion, f32[384,512,1]{1,0,2:T(8,128)S(1)} %get-tuple-element.15, f32[384,512,1]{1,0,2:T(8,128)S(1)} %copy.121), kind=kOutput, calls=%fused_computation.7 | convolution fusion | flops 2420899840 | bytes 4718592 | tf_op jit(solution)/shard_map/kbr,bd->krd/dot_general | solution.py:68
  116.2 5.3 %fusion.20 = f32[512,128,2]{1,0,2:T(8,128)S(1)} fusion(f32[128,2,512]{2,0,1:T(8,128)S(1)} %get-tuple-element.8, f32[128,2,512]{2,0,1:T(8,128)S(1)} %get-tuple-element.7), kind=kOutput, calls=%fused_computation.38 | convolution fusion | flops 809107456 | bytes 1572864 | tf_op jit(solution)/shard_map/krd,db->kbr/dot_general | solution.py:78
  121.5 5.1 %convolution_add_fusion.3 = f32[512,128,2]{1,0,2:T(8,128)S(1)} fusion(f32[512,128,2]{1,0,2:T(8,128)S(1)} %fusion.20, f32[128,2,512]{2,0,1:T(8,128)S(1)} %get-tuple-element.8), kind=kOutput, calls=%fused_computation.14 | convolution fusion | flops 809369600 | bytes 1572864 | tf_op jit(solution)/shard_map/krd,db->kbr/dot_general | solution.py:81
  126.6 6.0 %add_bitcast_fusion.1 = (f32[128,512,2]{0,1,2:T(8,128)S(1)}, f32[128,512,2]{0,1,2:T(8,128)S(1)}) fusion(f32[512,128,2]{1,0,2:T(8,128)S(1)} %convolution_add_fusion.3, f32[512,2]{0,1:T(2,128)S(1)} %get-tuple-element.28, f32[512,2]{0,1:T(2,128)S(1)} %get-tuple-element.27, f32[512,128,2]{1,0,2:T(8,128)S(1)} %fusion.20, f32[128,2,512]{2,0,1:T(8,128)S(1)} %get-tuple-element.7), kind=kOutput, calls=%fused_computation.57 | convolution fusion | flops 810156032 | bytes 2629632 | tf_op jit(solution)/shard_map/krd,db->kbr/dot_general | solution.py:82
  133.4 13.2 %all_to_all.237 = f32[128,512,1]{0,2,1:T(1,128)S(1)} all-to-all(f32[128,512,1]{0,2,1:T(1,128)S(1)} %bitcast.205), channel_id=1, replica_groups=mesh['seq'=16,'chan'=2] {'seq'}, dimensions={1} | all-to-all | bytes 524288 | tf_op jit(solution)/shard_map/all_to_all | solution.py:96
  146.7 3.9 %all-to-all-start.6 = ((f32[128,512,1]{0,2,1:T(1,128)}), f32[128,512,1]{0,2,1:T(1,128)S(1)}, u32[]{:S(2)}, u32[]{:S(2)}) async-start(f32[128,512,1]{0,2,1:T(1,128)} %bitcast.36), calls=%async_computation.6 | async-start | bytes 524288 | tf_op jit(solution)/shard_map/all_to_all | solution.py:99
  151.2 8.4 %all-to-all-done.6 = f32[128,512,1]{0,2,1:T(1,128)S(1)} async-done(((f32[128,512,1]{0,2,1:T(1,128)}), f32[128,512,1]{0,2,1:T(1,128)S(1)}, u32[]{:S(2)}, u32[]{:S(2)}) %all-to-all-start.6) | async-done | bytes 262176 | tf_op jit(solution)/shard_map/all_to_all | solution.py:99
  164.7 8.8 %all-to-all-done.7 = f32[128,32,16]{0,1,2:T(8,128)S(1)} async-done(((f32[128,32,16]{0,1,2:T(8,128)}), f32[128,32,16]{0,1,2:T(8,128)S(1)}, u32[]{:S(2)}, u32[]{:S(2)}) %all-to-all-start.7) | async-done | bytes 262176 | tf_op jit(solution)/shard_map/all_to_all | solution.py:130
  173.6 12.4 %all_to_all.238 = f32[128,512,1]{0,2,1:T(1,128)S(1)} all-to-all(f32[128,512,1]{0,2,1:T(1,128)S(1)} %bitcast.203), channel_id=1, replica_groups=mesh['seq'=16,'chan'=2] {'seq'}, dimensions={1} | all-to-all | bytes 524288 | tf_op jit(solution)/shard_map/all_to_all | solution.py:156
  192.4 8.3 %all-to-all-done.10 = f32[128,32,16]{0,1,2:T(8,128)S(1)} async-done(((f32[128,32,16]{0,1,2:T(8,128)}), f32[128,32,16]{0,1,2:T(8,128)S(1)}, u32[]{:S(2)}, u32[]{:S(2)}) %all-to-all-start.10) | async-done | bytes 262176 | tf_op jit(solution)/shard_map/all_to_all | solution.py:50
  204.4 8.9 %all-to-all-done.9 = f32[128,32,16]{0,1,2:T(8,128)S(1)} async-done(((f32[128,32,16]{0,1,2:T(8,128)}), f32[128,32,16]{0,1,2:T(8,128)S(1)}, u32[]{:S(2)}, u32[]{:S(2)}) %all-to-all-start.9) | async-done | bytes 262176 | tf_op jit(solution)/shard_map/all_to_all | solution.py:49
  213.3 5.6 %fusion.15 = f32[128,2,512]{2,0,1:T(8,128)S(1)} fusion(f32[128,512,1]{0,1,2:T(8,128)S(1)} %get-tuple-element.26, f32[128,512,1]{0,1,2:T(8,128)S(1)} %get-tuple-element.25, f32[128,512,1]{0,1,2:T(8,128)S(1)} %get-tuple-element.24, f32[128,512,1]{0,1,2:T(8,128)S(1)} %bitcast.217), kind=kOutput, calls=%fused_computation.33 | convolution fusion | flops 809369600 | bytes 1572864 | tf_op jit(solution)/shard_map/kbr,bd->krd/dot_general | solution.py:67
  218.9 6.3 %convolution_subtract_fusion.2 = f32[128,2,512]{2,0,1:T(8,128)S(1)} fusion(f32[128,2,512]{2,0,1:T(8,128)S(1)} %fusion.15, f32[128,512,1]{0,1,2:T(8,128)S(1)} %get-tuple-element.26, f32[128,512,1]{0,1,2:T(8,128)S(1)} %get-tuple-element.25), kind=kOutput, calls=%fused_computation.13 | convolution fusion | flops 809500672 | bytes 1572864 | tf_op jit(solution)/shard_map/kbr,bd->krd/dot_general | solution.py:69
  225.2 7.1 %multiply_add_fusion.1 = (f32[128,2,512]{2,0,1:T(8,128)S(1)}, f32[128,2,512]{2,0,1:T(8,128)S(1)}) fusion(f32[128,2,512]{2,0,1:T(8,128)S(1)} %convolution_subtract_fusion.2, f32[384,2,512]{2,0,1:T(8,128)} %copy-done.1, f32[384,2,512]{2,0,1:T(8,128)S(1)} %convolution_subtract_fusion, f32[128,2,512]{2,0,1:T(8,128)S(1)} %fusion.15, ...), kind=kOutput, calls=%fused_computation.54 | convolution fusion | flops 810549248 | bytes 3670016 | tf_op jit(solution)/shard_map/kbr,bd->krd/dot_general | solution.py:68
  232.3 4.8 %fusion.18 = f32[512,128,2]{1,0,2:T(8,128)S(1)} fusion(f32[128,2,512]{2,0,1:T(8,128)S(1)} %get-tuple-element.6, f32[128,2,512]{2,0,1:T(8,128)S(1)} %get-tuple-element.5), kind=kOutput, calls=%fused_computation.36 | convolution fusion | flops 809107456 | bytes 1572864 | tf_op jit(solution)/shard_map/krd,db->kbr/dot_general | solution.py:78
  237.2 5.3 %convolution_add_fusion.1 = f32[512,128,2]{1,0,2:T(8,128)S(1)} fusion(f32[512,128,2]{1,0,2:T(8,128)S(1)} %fusion.18, f32[128,2,512]{2,0,1:T(8,128)S(1)} %get-tuple-element.6), kind=kOutput, calls=%fused_computation.10 | convolution fusion | flops 809369600 | bytes 1572864 | tf_op jit(solution)/shard_map/krd,db->kbr/dot_general | solution.py:81
  242.5 5.2 %add_bitcast_fusion = (f32[128,512,2]{0,1,2:T(8,128)S(1)}, f32[128,512,2]{0,1,2:T(8,128)S(1)}) fusion(f32[512,128,2]{1,0,2:T(8,128)S(1)} %convolution_add_fusion.1, f32[512,2]{0,1:T(2,128)S(1)} %get-tuple-element.28, f32[512,2]{0,1:T(2,128)S(1)} %get-tuple-element.27, f32[512,128,2]{1,0,2:T(8,128)S(1)} %fusion.18, f32[128,2,512]{2,0,1:T(8,128)S(1)} %get-tuple-element.5), kind=kOutput, calls=%fused_computation.51 | convolution fusion | flops 810156032 | bytes 2629632 | tf_op jit(solution)/shard_map/krd,db->kbr/dot_general | solution.py:82
  248.5 12.4 %all_to_all.239 = f32[128,512,1]{0,2,1:T(1,128)S(1)} all-to-all(f32[128,512,1]{0,2,1:T(1,128)S(1)} %bitcast.204), channel_id=1, replica_groups=mesh['seq'=16,'chan'=2] {'seq'}, dimensions={1} | all-to-all | bytes 524288 | tf_op jit(solution)/shard_map/all_to_all | solution.py:96
  260.9 3.7 %all-to-all-start.12 = ((f32[128,512,1]{0,2,1:T(1,128)}), f32[128,512,1]{0,2,1:T(1,128)S(1)}, u32[]{:S(2)}, u32[]{:S(2)}) async-start(f32[128,512,1]{0,2,1:T(1,128)} %bitcast.69), calls=%async_computation.12 | async-start | bytes 524288 | tf_op jit(solution)/shard_map/all_to_all | solution.py:99
  265.1 8.5 %all-to-all-done.12 = f32[128,512,1]{0,2,1:T(1,128)S(1)} async-done(((f32[128,512,1]{0,2,1:T(1,128)}), f32[128,512,1]{0,2,1:T(1,128)S(1)}, u32[]{:S(2)}, u32[]{:S(2)}) %all-to-all-start.12) | async-done | bytes 262176 | tf_op jit(solution)/shard_map/all_to_all | solution.py:99
  278.7 8.9 %all-to-all-done.13 = f32[128,32,16]{0,1,2:T(8,128)S(1)} async-done(((f32[128,32,16]{0,1,2:T(8,128)}), f32[128,32,16]{0,1,2:T(8,128)S(1)}, u32[]{:S(2)}, u32[]{:S(2)}) %all-to-all-start.13) | async-done | bytes 262176 | tf_op jit(solution)/shard_map/all_to_all | solution.py:130
  (69 shorter events, 42.8 us)
Async XLA Ops:
  0.0 289.7 %copy-start = (bf16[256,128]{1,0:T(8,128)(2,1)S(1)}, bf16[256,128]{1,0:T(8,128)(2,1)}, u32[]{:S(2)}) copy-start(bf16[256,128]{1,0:T(8,128)(2,1)} %param.15) | copy-start | bytes 196612
  0.0 23.4 %copy-start.3 = (f32[128,512]{1,0:T(8,128)S(1)}, f32[128,512]{1,0:T(8,128)}, u32[]{:S(2)}) copy-start(f32[128,512]{1,0:T(8,128)} %param.11) | copy-start | bytes 786436
  3.7 16.1 %all-to-all-start = ((bf16[16,2,2048]{2,1,0:T(2,128)(2,1)}), bf16[16,2,2048]{2,1,0:T(2,128)(2,1)S(1)}, u32[]{:S(2)}, u32[]{:S(2)}) async-start(bf16[16,2,2048]{2,1,0:T(2,128)(2,1)} %reshape.345), calls=%async_computation | async-start | bytes 262144 | tf_op jit(solution)/shard_map/all_to_all | solution.py:133
  19.9 12.0 %all-to-all-start.2 = ((f32[128,512,1]{0,2,1:T(1,128)}), f32[128,512,1]{0,2,1:T(1,128)S(1)}, u32[]{:S(2)}, u32[]{:S(2)}) async-start(f32[128,512,1]{0,2,1:T(1,128)} %bitcast.9), calls=%async_computation.2 | async-start | bytes 524288 | tf_op jit(solution)/shard_map/all_to_all | solution.py:136
  31.9 12.7 %all-to-all-start.1 = ((f32[128,512,1]{0,2,1:T(1,128)}), f32[128,512,1]{0,2,1:T(1,128)S(1)}, u32[]{:S(2)}, u32[]{:S(2)}) async-start(f32[128,512,1]{0,2,1:T(1,128)} %bitcast.5), calls=%async_computation.1 | async-start | bytes 524288 | tf_op jit(solution)/shard_map/all_to_all | solution.py:135
  47.9 22.5 %all-to-all-start.4 = ((f32[384,32,16]{0,1,2:T(8,128)}), f32[384,32,16]{0,1,2:T(8,128)S(1)}, u32[]{:S(2)}, u32[]{:S(2)}) async-start(f32[384,32,16]{0,1,2:T(8,128)} %copy.119), calls=%async_computation.4 | async-start | bytes 1572864 | tf_op jit(solution)/shard_map/all_to_all | solution.py:50
  70.4 23.6 %all-to-all-start.3 = ((f32[384,32,16]{0,1,2:T(8,128)}), f32[384,32,16]{0,1,2:T(8,128)S(1)}, u32[]{:S(2)}, u32[]{:S(2)}) async-start(f32[384,32,16]{0,1,2:T(8,128)} %copy.118), calls=%async_computation.3 | async-start | bytes 1572864 | tf_op jit(solution)/shard_map/all_to_all | solution.py:49
  115.0 1.2 copy-start.1
  146.7 17.8 %copy-start.2 = (bf16[128,512]{1,0:T(8,128)(2,1)S(1)}, bf16[128,512]{1,0:T(8,128)(2,1)}, u32[]{:S(2)}) copy-start(bf16[128,512]{1,0:T(8,128)(2,1)} %param.8) | copy-start | bytes 393220
  146.7 17.9 %copy-start.4 = (bf16[128,512]{1,0:T(8,128)(2,1)S(1)}, bf16[128,512]{1,0:T(8,128)(2,1)}, u32[]{:S(2)}) copy-start(bf16[128,512]{1,0:T(8,128)(2,1)} %param.9) | copy-start | bytes 393220
  146.7 12.9 %all-to-all-start.6 = ((f32[128,512,1]{0,2,1:T(1,128)}), f32[128,512,1]{0,2,1:T(1,128)S(1)}, u32[]{:S(2)}, u32[]{:S(2)}) async-start(f32[128,512,1]{0,2,1:T(1,128)} %bitcast.36), calls=%async_computation.6 | async-start | bytes 524288 | tf_op jit(solution)/shard_map/all_to_all | solution.py:99
  150.6 23.0 %copy-start.6 = (f32[128]{0:T(128)S(1)}, f32[128]{0:T(128)}, u32[]{:S(2)}) copy-start(f32[128]{0:T(128)} %param.13) | copy-start | bytes 1540
  160.9 12.7 %all-to-all-start.7 = ((f32[128,32,16]{0,1,2:T(8,128)}), f32[128,32,16]{0,1,2:T(8,128)S(1)}, u32[]{:S(2)}, u32[]{:S(2)}) async-start(f32[128,32,16]{0,1,2:T(8,128)} %copy.131), calls=%async_computation.7 | async-start | bytes 524288 | tf_op jit(solution)/shard_map/all_to_all | solution.py:130
  188.0 12.6 %all-to-all-start.10 = ((f32[128,32,16]{0,1,2:T(8,128)}), f32[128,32,16]{0,1,2:T(8,128)S(1)}, u32[]{:S(2)}, u32[]{:S(2)}) async-start(f32[128,32,16]{0,1,2:T(8,128)} %copy.138), calls=%async_computation.10 | async-start | bytes 524288 | tf_op jit(solution)/shard_map/all_to_all | solution.py:50
  200.7 12.6 %all-to-all-start.9 = ((f32[128,32,16]{0,1,2:T(8,128)}), f32[128,32,16]{0,1,2:T(8,128)S(1)}, u32[]{:S(2)}, u32[]{:S(2)}) async-start(f32[128,32,16]{0,1,2:T(8,128)} %copy.137), calls=%async_computation.9 | async-start | bytes 524288 | tf_op jit(solution)/shard_map/all_to_all | solution.py:49
  260.9 17.7 %copy-start.5 = (bf16[128,512]{1,0:T(8,128)(2,1)S(1)}, bf16[128,512]{1,0:T(8,128)(2,1)}, u32[]{:S(2)}) copy-start(bf16[128,512]{1,0:T(8,128)(2,1)} %param.10) | copy-start | bytes 393220
  260.9 26.7 %copy-start.7 = (f32[128]{0:T(128)S(1)}, f32[128]{0:T(128)}, u32[]{:S(2)}) copy-start(f32[128]{0:T(128)} %param.14) | copy-start | bytes 1540
  260.9 12.8 %all-to-all-start.12 = ((f32[128,512,1]{0,2,1:T(1,128)}), f32[128,512,1]{0,2,1:T(1,128)S(1)}, u32[]{:S(2)}, u32[]{:S(2)}) async-start(f32[128,512,1]{0,2,1:T(1,128)} %bitcast.69), calls=%async_computation.12 | async-start | bytes 524288 | tf_op jit(solution)/shard_map/all_to_all | solution.py:99
  275.0 12.6 %all-to-all-start.13 = ((f32[128,32,16]{0,1,2:T(8,128)}), f32[128,32,16]{0,1,2:T(8,128)S(1)}, u32[]{:S(2)}, u32[]{:S(2)}) async-start(f32[128,32,16]{0,1,2:T(8,128)} %copy.149), calls=%async_computation.13 | async-start | bytes 524288 | tf_op jit(solution)/shard_map/all_to_all | solution.py:130
where the time goes:
time: 297 us; the launch traced here: 291 us
  waiting for transfers between devices  110 us (37%)
  matrix products  76.8 us (26%)
  starting transfers between devices  46.1 us (16%)
  blocking collectives  40.1 us (14%)
  local copies, waits for them, and re-layouts  13.5 us (5%)
  other arithmetic  4.12 us (1%)
    all_to_all x2, waiting for transfers between devices, spectra(): lax.all_to_all(real_twist, 'seq', split_axis=2, concat_axis=1, tiled=True)  26.8 us
    all_to_all x2, waiting for transfers between devices, spectra(): lax.all_to_all(imag_twist, 'seq', split_axis=2, concat_axis=1, tiled=True)  26 us
    all_to_all x2, blocking collectives, inverse(): lax.all_to_all(real_twist[:, :, :row_count], 'seq', split_axis=1, concat_...  25.6 us
    all_to_all x2, waiting for transfers between devices, to_tokens(): lax.all_to_all(result_cols, 'seq', split_axis=2, concat_axis=1, tiled=True)  17.8 us
    all_to_all x2, waiting for transfers between devices, inverse(): lax.all_to_all(imag_send, 'seq', split_axis=1, concat_axis=2, tiled=True)  17 us
    dot_general x2, matrix products, spectra(): jnp.einsum('kbr,bd->krd', real_recv, -sine_q - cosine_q, precision=exact_...  14 us
    dot_general x2, matrix products, spectra(): jnp.einsum('kbr,bd->krd', imag_recv, cosine_q - sine_q, precision=exact_m...  13.4 us
    all_to_all x1, blocking collectives, per_device(): lax.all_to_all(columns(gated), 'seq', split_axis=1, concat_axis=2, tiled=...  12.4 us
  transfers between devices with their start and end apart: 11, of which 11 were waited for; matrix products, arithmetic and copies ran while one was open for 2% of the time, Pallas kernels for 0%

commit v1 on v0

--- a/solution.py
+++ b/solution.py
@@ -127,7 +127,12 @@
 
     def to_tokens(result_cols):
         return from_columns(
-            lax.all_to_all(result_cols, "seq", split_axis=2, concat_axis=1, tiled=True)
+            jnp.concatenate(
+                lax.all_to_all(
+                    jnp.stack(jnp.split(result_cols, lax.axis_size("seq"), axis=2)), "seq", 0, 0
+                ),
+                axis=1,
+            )
         )
 
     values_cols = lax.all_to_all(columns(values), "seq", split_axis=1, concat_axis=2, tiled=True)

time: 297 us -> 314 us (1.057)
  local copies, waits for them, and re-layouts: 13.5 us -> 31.6 us
    unnamed x24 -> x54, local copies, waits for them, and re-layouts: 5.27 us -> 23.3 us
where the time goes in v1:
time: 314 us; the launch traced here: 309 us
  waiting for transfers between devices  110 us (35%)
  matrix products  77 us (25%)
  starting transfers between devices  45.8 us (15%)
  blocking collectives  40.1 us (13%)
  local copies, waits for them, and re-layouts  31.6 us (10%)
  other arithmetic  4.1 us (1%)
    all_to_all x2, waiting for transfers between devices, spectra(): lax.all_to_all(real_twist, 'seq', split_axis=2, concat_axis=1, tiled=True)  26.8 us
    all_to_all x2, waiting for transfers between devices, spectra(): lax.all_to_all(imag_twist, 'seq', split_axis=2, concat_axis=1, tiled=True)  26 us
    all_to_all x2, blocking collectives, inverse(): lax.all_to_all(real_twist[:, :, :row_count], 'seq', split_axis=1, concat_...  25.6 us
    unnamed x54, local copies, waits for them, and re-layouts  23.3 us
    all_to_all x2, waiting for transfers between devices, to_tokens(): lax.all_to_all(jnp.stack(jnp.split(result_cols, lax.axis_size('seq'), axi...  17.8 us
    all_to_all x2, waiting for transfers between devices, inverse(): lax.all_to_all(imag_send, 'seq', split_axis=1, concat_axis=2, tiled=True)  16.9 us
    dot_general x2, matrix products, spectra(): jnp.einsum('kbr,bd->krd', real_recv, -sine_q - cosine_q, precision=exact_...  14 us
    dot_general x2, matrix products, spectra(): jnp.einsum('kbr,bd->krd', imag_recv, cosine_q - sine_q, precision=exact_m...  13.4 us
  transfers between devices with their start and end apart: 11, of which 11 were waited for; matrix products, arithmetic and copies ran while one was open for 2% of the time, Pallas kernels for 0%

profile of v1, /device:TPU:0, one launch (start us, length us, event | category | flops | bytes accessed | tf_op | source)
XLA Modules:
  0.0 308.9 jit_solution(7363179672169133475)
XLA Ops:
  3.7 8.3 %all-to-all-start = ((bf16[16,2,2048]{2,1,0:T(2,128)(2,1)}), bf16[16,2,2048]{2,1,0:T(2,128)(2,1)S(1)}, u32[]{:S(2)}, u32[]{:S(2)}) async-start(bf16[16,2,2048]{2,1,0:T(2,128)(2,1)} %reshape.351), calls=%async_computation | async-start | bytes 262144 | tf_op jit(solution)/shard_map/all_to_all | solution.py:138
  13.9 6.0 %all-to-all-done = bf16[16,2,2048]{2,1,0:T(2,128)(2,1)S(1)} async-done(((bf16[16,2,2048]{2,1,0:T(2,128)(2,1)}), bf16[16,2,2048]{2,1,0:T(2,128)(2,1)S(1)}, u32[]{:S(2)}, u32[]{:S(2)}) %all-to-all-start) | async-done | bytes 131104 | tf_op jit(solution)/shard_map/all_to_all | solution.py:138
  24.3 7.6 %all-to-all-done.2 = f32[128,512,1]{0,2,1:T(1,128)S(1)} async-done(((f32[128,512,1]{0,2,1:T(1,128)}), f32[128,512,1]{0,2,1:T(1,128)S(1)}, u32[]{:S(2)}, u32[]{:S(2)}) %all-to-all-start.2) | async-done | bytes 262176 | tf_op jit(solution)/shard_map/all_to_all | solution.py:141
  31.9 3.7 %all-to-all-start.1 = ((f32[128,512,1]{0,2,1:T(1,128)}), f32[128,512,1]{0,2,1:T(1,128)S(1)}, u32[]{:S(2)}, u32[]{:S(2)}) async-start(f32[128,512,1]{0,2,1:T(1,128)} %bitcast.5), calls=%async_computation.1 | async-start | bytes 524288 | tf_op jit(solution)/shard_map/all_to_all | solution.py:140
  36.2 8.4 %all-to-all-done.1 = f32[128,512,1]{0,2,1:T(1,128)S(1)} async-done(((f32[128,512,1]{0,2,1:T(1,128)}), f32[128,512,1]{0,2,1:T(1,128)S(1)}, u32[]{:S(2)}, u32[]{:S(2)}) %all-to-all-start.1) | async-done | bytes 262176 | tf_op jit(solution)/shard_map/all_to_all | solution.py:140
  47.9 3.6 %all-to-all-start.4 = ((f32[384,32,16]{0,1,2:T(8,128)}), f32[384,32,16]{0,1,2:T(8,128)S(1)}, u32[]{:S(2)}, u32[]{:S(2)}) async-start(f32[384,32,16]{0,1,2:T(8,128)} %copy.206), calls=%async_computation.4 | async-start | bytes 1572864 | tf_op jit(solution)/shard_map/all_to_all | solution.py:50
  52.6 17.7 %all-to-all-done.4 = f32[384,32,16]{0,1,2:T(8,128)S(1)} async-done(((f32[384,32,16]{0,1,2:T(8,128)}), f32[384,32,16]{0,1,2:T(8,128)S(1)}, u32[]{:S(2)}, u32[]{:S(2)}) %all-to-all-start.4) | async-done | bytes 786464 | tf_op jit(solution)/shard_map/all_to_all | solution.py:50
  70.4 5.1 %all-to-all-start.3 = ((f32[384,32,16]{0,1,2:T(8,128)}), f32[384,32,16]{0,1,2:T(8,128)S(1)}, u32[]{:S(2)}, u32[]{:S(2)}) async-start(f32[384,32,16]{0,1,2:T(8,128)} %copy.205), calls=%async_computation.3 | async-start | bytes 1572864 | tf_op jit(solution)/shard_map/all_to_all | solution.py:49
  76.1 17.9 %all-to-all-done.3 = f32[384,32,16]{0,1,2:T(8,128)S(1)} async-done(((f32[384,32,16]{0,1,2:T(8,128)}), f32[384,32,16]{0,1,2:T(8,128)S(1)}, u32[]{:S(2)}, u32[]{:S(2)}) %all-to-all-start.3) | async-done | bytes 786464 | tf_op jit(solution)/shard_map/all_to_all | solution.py:49
  94.5 6.5 %fusion = f32[384,2,512]{2,0,1:T(8,128)S(1)} fusion(f32[384,512,1]{1,0,2:T(8,128)S(1)} %get-tuple-element.16, f32[384,512,1]{1,0,2:T(8,128)S(1)} %get-tuple-element.17, f32[384,512,1]{1,0,2:T(8,128)S(1)} %get-tuple-element.15, f32[384,512,1]{1,0,2:T(8,128)S(1)} %copy.208), kind=kOutput, calls=%fused_computation.2 | convolution fusion | flops 2420768768 | bytes 4718592 | tf_op jit(solution)/shard_map/kbr,bd->krd/dot_general | solution.py:67
  101.0 7.1 %convolution_subtract_fusion = f32[384,2,512]{2,0,1:T(8,128)S(1)} fusion(f32[384,2,512]{2,0,1:T(8,128)S(1)} %fusion, f32[384,512,1]{1,0,2:T(8,128)S(1)} %get-tuple-element.16, f32[384,512,1]{1,0,2:T(8,128)S(1)} %get-tuple-element.17), kind=kOutput, calls=%fused_computation.8 | convolution fusion | flops 2420637696 | bytes 4718592 | tf_op jit(solution)/shard_map/kbr,bd->krd/dot_general | solution.py:69
  108.1 6.9 %convolution_add_fusion = f32[384,2,512]{2,0,1:T(8,128)S(1)} fusion(f32[384,2,512]{2,0,1:T(8,128)S(1)} %fusion, f32[384,512,1]{1,0,2:T(8,128)S(1)} %get-tuple-element.15, f32[384,512,1]{1,0,2:T(8,128)S(1)} %copy.208), kind=kOutput, calls=%fused_computation.7 | convolution fusion | flops 2420899840 | bytes 4718592 | tf_op jit(solution)/shard_map/kbr,bd->krd/dot_general | solution.py:68
  116.2 5.3 %fusion.20 = f32[512,128,2]{1,0,2:T(8,128)S(1)} fusion(f32[128,2,512]{2,0,1:T(8,128)S(1)} %get-tuple-element.8, f32[128,2,512]{2,0,1:T(8,128)S(1)} %get-tuple-element.7), kind=kOutput, calls=%fused_computation.38 | convolution fusion | flops 809107456 | bytes 1572864 | tf_op jit(solution)/shard_map/krd,db->kbr/dot_general | solution.py:78
  121.5 5.1 %convolution_add_fusion.3 = f32[512,128,2]{1,0,2:T(8,128)S(1)} fusion(f32[512,128,2]{1,0,2:T(8,128)S(1)} %fusion.20, f32[128,2,512]{2,0,1:T(8,128)S(1)} %get-tuple-element.8), kind=kOutput, calls=%fused_computation.14 | convolution fusion | flops 809369600 | bytes 1572864 | tf_op jit(solution)/shard_map/krd,db->kbr/dot_general | solution.py:81
  126.6 6.2 %add_bitcast_fusion.1 = (f32[128,512,2]{0,1,2:T(8,128)S(1)}, f32[128,512,2]{0,1,2:T(8,128)S(1)}) fusion(f32[512,128,2]{1,0,2:T(8,128)S(1)} %convolution_add_fusion.3, f32[512,2]{0,1:T(2,128)S(1)} %get-tuple-element.60, f32[512,2]{0,1:T(2,128)S(1)} %get-tuple-element.59, f32[512,128,2]{1,0,2:T(8,128)S(1)} %fusion.20, f32[128,2,512]{2,0,1:T(8,128)S(1)} %get-tuple-element.7), kind=kOutput, calls=%fused_computation.57 | convolution fusion | flops 810156032 | bytes 2629632 | tf_op jit(solution)/shard_map/krd,db->kbr/dot_general | solution.py:82
  133.6 13.2 %all_to_all.217 = f32[128,512,1]{0,2,1:T(1,128)S(1)} all-to-all(f32[128,512,1]{0,2,1:T(1,128)S(1)} %bitcast.291), channel_id=1, replica_groups=mesh['seq'=16,'chan'=2] {'seq'}, dimensions={1} | all-to-all | bytes 524288 | tf_op jit(solution)/shard_map/all_to_all | solution.py:96
  146.8 3.8 %all-to-all-start.6 = ((f32[128,512,1]{0,2,1:T(1,128)}), f32[128,512,1]{0,2,1:T(1,128)S(1)}, u32[]{:S(2)}, u32[]{:S(2)}) async-start(f32[128,512,1]{0,2,1:T(1,128)} %bitcast.36), calls=%async_computation.6 | async-start | bytes 524288 | tf_op jit(solution)/shard_map/all_to_all | solution.py:99
  151.2 8.4 %all-to-all-done.6 = f32[128,512,1]{0,2,1:T(1,128)S(1)} async-done(((f32[128,512,1]{0,2,1:T(1,128)}), f32[128,512,1]{0,2,1:T(1,128)S(1)}, u32[]{:S(2)}, u32[]{:S(2)}) %all-to-all-start.6) | async-done | bytes 262176 | tf_op jit(solution)/shard_map/all_to_all | solution.py:99
  173.8 8.8 %all-to-all-done.7 = f32[16,128,32,1]{1,2,3,0:T(8,128)S(1)} async-done(((f32[16,128,32,1]{1,2,3,0:T(8,128)}), f32[16,128,32,1]{1,2,3,0:T(8,128)S(1)}, u32[]{:S(2)}, u32[]{:S(2)}) %all-to-all-start.7) | async-done | bytes 262176 | tf_op jit(solution)/shard_map/all_to_all | solution.py:131
  182.7 12.4 %all_to_all.218 = f32[128,512,1]{0,2,1:T(1,128)S(1)} all-to-all(f32[128,512,1]{0,2,1:T(1,128)S(1)} %bitcast.289), channel_id=1, replica_groups=mesh['seq'=16,'chan'=2] {'seq'}, dimensions={1} | all-to-all | bytes 524288 | tf_op jit(solution)/shard_map/all_to_all | solution.py:161
  197.1 3.5 %all-to-all-start.10 = ((f32[128,32,16]{0,1,2:T(8,128)}), f32[128,32,16]{0,1,2:T(8,128)S(1)}, u32[]{:S(2)}, u32[]{:S(2)}) async-start(f32[128,32,16]{0,1,2:T(8,128)} %copy.238), calls=%async_computation.10 | async-start | bytes 524288 | tf_op jit(solution)/shard_map/all_to_all | solution.py:50
  201.5 8.3 %all-to-all-done.10 = f32[128,32,16]{0,1,2:T(8,128)S(1)} async-done(((f32[128,32,16]{0,1,2:T(8,128)}), f32[128,32,16]{0,1,2:T(8,128)S(1)}, u32[]{:S(2)}, u32[]{:S(2)}) %all-to-all-start.10) | async-done | bytes 262176 | tf_op jit(solution)/shard_map/all_to_all | solution.py:50
  213.5 8.9 %all-to-all-done.9 = f32[128,32,16]{0,1,2:T(8,128)S(1)} async-done(((f32[128,32,16]{0,1,2:T(8,128)}), f32[128,32,16]{0,1,2:T(8,128)S(1)}, u32[]{:S(2)}, u32[]{:S(2)}) %all-to-all-start.9) | async-done | bytes 262176 | tf_op jit(solution)/shard_map/all_to_all | solution.py:49
  222.4 5.6 %fusion.15 = f32[128,2,512]{2,0,1:T(8,128)S(1)} fusion(f32[128,512,1]{0,1,2:T(8,128)S(1)} %get-tuple-element.42, f32[128,512,1]{0,1,2:T(8,128)S(1)} %get-tuple-element.41, f32[128,512,1]{0,1,2:T(8,128)S(1)} %get-tuple-element.40, f32[128,512,1]{0,1,2:T(8,128)S(1)} %bitcast.303), kind=kOutput, calls=%fused_computation.33 | convolution fusion | flops 809369600 | bytes 1572864 | tf_op jit(solution)/shard_map/kbr,bd->krd/dot_general | solution.py:67
  228.0 6.3 %convolution_subtract_fusion.2 = f32[128,2,512]{2,0,1:T(8,128)S(1)} fusion(f32[128,2,512]{2,0,1:T(8,128)S(1)} %fusion.15, f32[128,512,1]{0,1,2:T(8,128)S(1)} %get-tuple-element.42, f32[128,512,1]{0,1,2:T(8,128)S(1)} %get-tuple-element.41), kind=kOutput, calls=%fused_computation.13 | convolution fusion | flops 809500672 | bytes 1572864 | tf_op jit(solution)/shard_map/kbr,bd->krd/dot_general | solution.py:69
  234.3 7.1 %multiply_add_fusion.1 = (f32[128,2,512]{2,0,1:T(8,128)S(1)}, f32[128,2,512]{2,0,1:T(8,128)S(1)}) fusion(f32[128,2,512]{2,0,1:T(8,128)S(1)} %convolution_subtract_fusion.2, f32[384,2,512]{2,0,1:T(8,128)} %copy-done.1, f32[384,2,512]{2,0,1:T(8,128)S(1)} %convolution_subtract_fusion, f32[128,2,512]{2,0,1:T(8,128)S(1)} %fusion.15, ...), kind=kOutput, calls=%fused_computation.54 | convolution fusion | flops 810549248 | bytes 3670016 | tf_op jit(solution)/shard_map/kbr,bd->krd/dot_general | solution.py:68
  241.4 4.8 %fusion.18 = f32[512,128,2]{1,0,2:T(8,128)S(1)} fusion(f32[128,2,512]{2,0,1:T(8,128)S(1)} %get-tuple-element.6, f32[128,2,512]{2,0,1:T(8,128)S(1)} %get-tuple-element.5), kind=kOutput, calls=%fused_computation.36 | convolution fusion | flops 809107456 | bytes 1572864 | tf_op jit(solution)/shard_map/krd,db->kbr/dot_general | solution.py:78
  246.2 5.3 %convolution_add_fusion.1 = f32[512,128,2]{1,0,2:T(8,128)S(1)} fusion(f32[512,128,2]{1,0,2:T(8,128)S(1)} %fusion.18, f32[128,2,512]{2,0,1:T(8,128)S(1)} %get-tuple-element.6), kind=kOutput, calls=%fused_computation.10 | convolution fusion | flops 809369600 | bytes 1572864 | tf_op jit(solution)/shard_map/krd,db->kbr/dot_general | solution.py:81
  251.6 5.2 %add_bitcast_fusion = (f32[128,512,2]{0,1,2:T(8,128)S(1)}, f32[128,512,2]{0,1,2:T(8,128)S(1)}) fusion(f32[512,128,2]{1,0,2:T(8,128)S(1)} %convolution_add_fusion.1, f32[512,2]{0,1:T(2,128)S(1)} %get-tuple-element.60, f32[512,2]{0,1:T(2,128)S(1)} %get-tuple-element.59, f32[512,128,2]{1,0,2:T(8,128)S(1)} %fusion.18, f32[128,2,512]{2,0,1:T(8,128)S(1)} %get-tuple-element.5), kind=kOutput, calls=%fused_computation.51 | convolution fusion | flops 810156032 | bytes 2629632 | tf_op jit(solution)/shard_map/krd,db->kbr/dot_general | solution.py:82
  257.5 12.4 %all_to_all.219 = f32[128,512,1]{0,2,1:T(1,128)S(1)} all-to-all(f32[128,512,1]{0,2,1:T(1,128)S(1)} %bitcast.290), channel_id=1, replica_groups=mesh['seq'=16,'chan'=2] {'seq'}, dimensions={1} | all-to-all | bytes 524288 | tf_op jit(solution)/shard_map/all_to_all | solution.py:96
  274.1 8.5 %all-to-all-done.12 = f32[128,512,1]{0,2,1:T(1,128)S(1)} async-done(((f32[128,512,1]{0,2,1:T(1,128)}), f32[128,512,1]{0,2,1:T(1,128)S(1)}, u32[]{:S(2)}, u32[]{:S(2)}) %all-to-all-start.12) | async-done | bytes 262176 | tf_op jit(solution)/shard_map/all_to_all | solution.py:99
  296.6 8.9 %all-to-all-done.13 = f32[16,128,32,1]{1,2,3,0:T(8,128)S(1)} async-done(((f32[16,128,32,1]{1,2,3,0:T(8,128)}), f32[16,128,32,1]{1,2,3,0:T(8,128)S(1)}, u32[]{:S(2)}, u32[]{:S(2)}) %all-to-all-start.13) | async-done | bytes 262176 | tf_op jit(solution)/shard_map/all_to_all | solution.py:131
  (101 shorter events, 60.9 us)
Async XLA Ops:
  0.0 307.7 %copy-start = (bf16[256,128]{1,0:T(8,128)(2,1)S(1)}, bf16[256,128]{1,0:T(8,128)(2,1)}, u32[]{:S(2)}) copy-start(bf16[256,128]{1,0:T(8,128)(2,1)} %param.15) | copy-start | bytes 196612
  0.0 23.4 %copy-start.3 = (f32[128,512]{1,0:T(8,128)S(1)}, f32[128,512]{1,0:T(8,128)}, u32[]{:S(2)}) copy-start(f32[128,512]{1,0:T(8,128)} %param.11) | copy-start | bytes 786436
  3.7 16.1 %all-to-all-start = ((bf16[16,2,2048]{2,1,0:T(2,128)(2,1)}), bf16[16,2,2048]{2,1,0:T(2,128)(2,1)S(1)}, u32[]{:S(2)}, u32[]{:S(2)}) async-start(bf16[16,2,2048]{2,1,0:T(2,128)(2,1)} %reshape.351), calls=%async_computation | async-start | bytes 262144 | tf_op jit(solution)/shard_map/all_to_all | solution.py:138
  19.9 12.0 %all-to-all-start.2 = ((f32[128,512,1]{0,2,1:T(1,128)}), f32[128,512,1]{0,2,1:T(1,128)S(1)}, u32[]{:S(2)}, u32[]{:S(2)}) async-start(f32[128,512,1]{0,2,1:T(1,128)} %bitcast.9), calls=%async_computation.2 | async-start | bytes 524288 | tf_op jit(solution)/shard_map/all_to_all | solution.py:141
  31.9 12.7 %all-to-all-start.1 = ((f32[128,512,1]{0,2,1:T(1,128)}), f32[128,512,1]{0,2,1:T(1,128)S(1)}, u32[]{:S(2)}, u32[]{:S(2)}) async-start(f32[128,512,1]{0,2,1:T(1,128)} %bitcast.5), calls=%async_computation.1 | async-start | bytes 524288 | tf_op jit(solution)/shard_map/all_to_all | solution.py:140
  47.9 22.5 %all-to-all-start.4 = ((f32[384,32,16]{0,1,2:T(8,128)}), f32[384,32,16]{0,1,2:T(8,128)S(1)}, u32[]{:S(2)}, u32[]{:S(2)}) async-start(f32[384,32,16]{0,1,2:T(8,128)} %copy.206), calls=%async_computation.4 | async-start | bytes 1572864 | tf_op jit(solution)/shard_map/all_to_all | solution.py:50
  70.4 23.6 %all-to-all-start.3 = ((f32[384,32,16]{0,1,2:T(8,128)}), f32[384,32,16]{0,1,2:T(8,128)S(1)}, u32[]{:S(2)}, u32[]{:S(2)}) async-start(f32[384,32,16]{0,1,2:T(8,128)} %copy.205), calls=%async_computation.3 | async-start | bytes 1572864 | tf_op jit(solution)/shard_map/all_to_all | solution.py:49
  115.0 1.2 copy-start.1
  146.8 12.8 %all-to-all-start.6 = ((f32[128,512,1]{0,2,1:T(1,128)}), f32[128,512,1]{0,2,1:T(1,128)S(1)}, u32[]{:S(2)}, u32[]{:S(2)}) async-start(f32[128,512,1]{0,2,1:T(1,128)} %bitcast.36), calls=%async_computation.6 | async-start | bytes 524288 | tf_op jit(solution)/shard_map/all_to_all | solution.py:99
  150.6 22.9 %copy-start.2 = (bf16[128,512]{1,0:T(8,128)(2,1)S(1)}, bf16[128,512]{1,0:T(8,128)(2,1)}, u32[]{:S(2)}) copy-start(bf16[128,512]{1,0:T(8,128)(2,1)} %param.8) | copy-start | bytes 393220
  150.6 23.1 %copy-start.4 = (bf16[128,512]{1,0:T(8,128)(2,1)S(1)}, bf16[128,512]{1,0:T(8,128)(2,1)}, u32[]{:S(2)}) copy-start(bf16[128,512]{1,0:T(8,128)(2,1)} %param.9) | copy-start | bytes 393220
  151.2 31.5 %copy-start.6 = (f32[128]{0:T(128)S(1)}, f32[128]{0:T(128)}, u32[]{:S(2)}) copy-start(f32[128]{0:T(128)} %param.13) | copy-start | bytes 1540
  170.0 12.7 %all-to-all-start.7 = ((f32[16,128,32,1]{1,2,3,0:T(8,128)}), f32[16,128,32,1]{1,2,3,0:T(8,128)S(1)}, u32[]{:S(2)}, u32[]{:S(2)}) async-start(f32[16,128,32,1]{1,2,3,0:T(8,128)} %constant_dynamic-update-slice_fusion), calls=%async_computation.7 | async-start | bytes 524288 | tf_op jit(solution)/shard_map/all_to_all | solution.py:131
  197.1 12.6 %all-to-all-start.10 = ((f32[128,32,16]{0,1,2:T(8,128)}), f32[128,32,16]{0,1,2:T(8,128)S(1)}, u32[]{:S(2)}, u32[]{:S(2)}) async-start(f32[128,32,16]{0,1,2:T(8,128)} %copy.238), calls=%async_computation.10 | async-start | bytes 524288 | tf_op jit(solution)/shard_map/all_to_all | solution.py:50
  209.7 12.6 %all-to-all-start.9 = ((f32[128,32,16]{0,1,2:T(8,128)}), f32[128,32,16]{0,1,2:T(8,128)S(1)}, u32[]{:S(2)}, u32[]{:S(2)}) async-start(f32[128,32,16]{0,1,2:T(8,128)} %copy.237), calls=%async_computation.9 | async-start | bytes 524288 | tf_op jit(solution)/shard_map/all_to_all | solution.py:49
  269.9 12.6 %all-to-all-start.12 = ((f32[128,512,1]{0,2,1:T(1,128)}), f32[128,512,1]{0,2,1:T(1,128)S(1)}, u32[]{:S(2)}, u32[]{:S(2)}) async-start(f32[128,512,1]{0,2,1:T(1,128)} %bitcast.83), calls=%async_computation.12 | async-start | bytes 524288 | tf_op jit(solution)/shard_map/all_to_all | solution.py:99
  273.5 23.0 %copy-start.5 = (bf16[128,512]{1,0:T(8,128)(2,1)S(1)}, bf16[128,512]{1,0:T(8,128)(2,1)}, u32[]{:S(2)}) copy-start(bf16[128,512]{1,0:T(8,128)(2,1)} %param.10) | copy-start | bytes 393220
  273.5 32.1 %copy-start.7 = (f32[128]{0:T(128)S(1)}, f32[128]{0:T(128)}, u32[]{:S(2)}) copy-start(f32[128]{0:T(128)} %param.14) | copy-start | bytes 1540
  293.0 12.6 %all-to-all-start.13 = ((f32[16,128,32,1]{1,2,3,0:T(8,128)}), f32[16,128,32,1]{1,2,3,0:T(8,128)S(1)}, u32[]{:S(2)}, u32[]{:S(2)}) async-start(f32[16,128,32,1]{1,2,3,0:T(8,128)} %constant_dynamic-update-slice_fusion.16), calls=%async_computation.13 | async-start | bytes 524288 | tf_op jit(solution)/shard_map/all_to_all | solution.py:131
